TPU v7x, 1024 devices: a whole 4x4x32 slice. The times are simulated.
1024 devices in a mesh: fsdp: 128 (over z_lo, y, core), tensor: 8 (over x, z_hi).
Axes of the slice: x: 4, y: 4, z: 32 (z_hi: 2, z_lo: 16; z = z_hi * 16 + z_lo), core: 2. Of those that a mesh axis runs over, the one named last changes fastest.
Arguments:
- new_hidden: bfloat16 [2048, 2, 8192], P('fsdp'), may hold values from -6 to 6
- new_queries: bfloat16 [2048, 2, 8192], P('fsdp', None, 'tensor'), may hold values from -540 to 540
- paged_cache: bfloat16 [4096, 64, 2048], P('fsdp', None, 'tensor'), may hold values from -6 to 6
- block_table: int32 [2048, 8], P('fsdp'), may hold values from 0 to 31
- lengths: int32 [2048], P('fsdp'), may hold values from 1 to 512
- destination: int32 [2048], P('fsdp'), may hold values from -1 to 127, as said below
- train_hidden: bfloat16 [8192, 8192], P('fsdp'), may hold values from -6 to 6
- train_queries: bfloat16 [8192, 8192], P('fsdp', 'tensor'), may hold values from -540 to 540
- documents: int32 [128, 64], P('fsdp'), may hold values from 0 to 3, never falling along the last dimension, each value on 1 to 32 neighbouring positions
- project_weight: bfloat16 [8192, 2048], P('fsdp', 'tensor'), may hold values from -0.0625 to 0.0625
- project_bias: float32 [2048], P('tensor'), may hold values from -3 to 3
Outputs:
- decoded: bfloat16 [2048, 2, 8192], P('fsdp', None, 'tensor')
- train_attention: bfloat16 [8192, 8192], P('fsdp', 'tensor')
- handover: bfloat16 [16384, 2, 2048], P('fsdp', None, 'tensor')
Inputs may be any that keep to these rules, and one draw needn't show every extreme that they name: `destination`: the rows of one fsdp index name each training shard at most once.
All inputs are finite; a program needn't handle non-finite values.
Results may differ from a plain program's by a relative error of at most 0.0095.
Values may be sent and summed in bfloat16 or wider, within the bound.
A program may use at most 64 MiB of HBM per device.

v0:
```python
import jax
import jax.numpy as jnp
from jax import lax
from jax.sharding import PartitionSpec as P

HEADS = 64
KV_HEADS = 8
HEAD_DIM = 128


masked_value = -1e30


def local(
    new_hidden,
    new_queries,
    paged_cache,
    block_table,
    lengths,
    destination,
    train_hidden,
    train_queries,
    documents,
    project_weight,
    project_bias,
):
    row_count = new_hidden.shape[0]
    model_width = new_hidden.shape[2]
    columns = project_weight.shape[1]
    local_kv = columns // (2 * HEAD_DIM)
    group_size = HEADS // KV_HEADS
    scaling = HEAD_DIM ** (-0.5)
    train_count = train_hidden.shape[0]
    flat_new = new_hidden.reshape(row_count * 2, model_width)
    gathered = lax.all_gather(project_weight, "fsdp", axis=0, tiled=True)
    decode_sum = jnp.dot(flat_new, gathered, preferred_element_type=jnp.float32)
    train_sum = jnp.dot(train_hidden, gathered, preferred_element_type=jnp.float32)
    fresh = (
        (decode_sum + project_bias)
        .astype(jnp.bfloat16)
        .reshape(row_count, 2, local_kv, 2, HEAD_DIM)
    )
    train_kv = (
        (train_sum + project_bias).astype(jnp.bfloat16).reshape(train_count, local_kv, 2, HEAD_DIM)
    )
    owners = lax.axis_size("fsdp")
    selector = (destination[None, :] == jnp.arange(owners, dtype=jnp.int32)[:, None]).astype(
        jnp.bfloat16
    )
    outgoing = jnp.dot(
        selector, fresh.reshape(row_count, 2 * columns), preferred_element_type=jnp.float32
    )
    outgoing = outgoing.astype(jnp.bfloat16).reshape(owners, 2, columns)
    handover = lax.all_to_all(outgoing, "fsdp", split_axis=0, concat_axis=0, tiled=True)
    context = paged_cache.shape[1] * block_table.shape[1]
    block_rows = 16
    count_blocks = row_count // block_rows
    order = jnp.arange(2, dtype=jnp.int32)
    allowed_new = order[None, :] <= order[:, None]
    places = jnp.arange(context, dtype=jnp.int32)

    def decode_block(operands):
        queries, tables, spans, fresh_rows = operands
        cached = jnp.take(paged_cache, tables, axis=0).reshape(
            block_rows, context, local_kv, 2, HEAD_DIM
        )
        heads_q = queries.reshape(block_rows, 2, local_kv, group_size, HEAD_DIM)
        old_scores = (
            jnp.einsum(
                "btkgd,bckd->btkgc",
                heads_q,
                cached[:, :, :, 0, :],
                preferred_element_type=jnp.float32,
            )
            * scaling
        )
        allowed_old = places[None, :] < spans[:, None]
        old_scores = jnp.where(allowed_old[:, None, None, None, :], old_scores, masked_value)
        new_scores = (
            jnp.einsum(
                "btkgd,bskd->btkgs",
                heads_q,
                fresh_rows[:, :, :, 0, :],
                preferred_element_type=jnp.float32,
            )
            * scaling
        )
        new_scores = jnp.where(allowed_new[None, :, None, None, :], new_scores, masked_value)
        highest = jnp.maximum(
            jnp.max(old_scores, -1, keepdims=True), jnp.max(new_scores, -1, keepdims=True)
        )
        old_exp = jnp.exp(old_scores - highest)
        new_exp = jnp.exp(new_scores - highest)
        totals = jnp.sum(old_exp, -1, keepdims=True) + jnp.sum(new_exp, -1, keepdims=True)
        old_weights = (old_exp / totals).astype(jnp.bfloat16)
        new_weights = (new_exp / totals).astype(jnp.bfloat16)
        result = jnp.einsum(
            "btkgc,bckd->btkgd",
            old_weights,
            cached[:, :, :, 1, :],
            preferred_element_type=jnp.float32,
        )
        result = result + jnp.einsum(
            "btkgs,bskd->btkgd",
            new_weights,
            fresh_rows[:, :, :, 1, :],
            preferred_element_type=jnp.float32,
        )
        return result.astype(jnp.bfloat16).reshape(block_rows, 2, local_kv * group_size * HEAD_DIM)

    decoded = lax.map(
        decode_block,
        (
            new_queries.reshape(count_blocks, block_rows, 2, new_queries.shape[2]),
            block_table.reshape(count_blocks, block_rows, block_table.shape[1]),
            lengths.reshape(count_blocks, block_rows),
            fresh.reshape(count_blocks, block_rows, 2, local_kv, 2, HEAD_DIM),
        ),
    )
    decoded = decoded.reshape(row_count, 2, new_queries.shape[2])
    doc_row = documents[0]
    train_places = jnp.arange(train_count, dtype=jnp.int32)
    allowed = (train_places[None, :] <= train_places[:, None]) & (
        doc_row[None, :] == doc_row[:, None]
    )
    heads_train = train_queries.reshape(train_count, local_kv, group_size, HEAD_DIM)
    scores = (
        jnp.einsum(
            "tkgd,skd->kgts", heads_train, train_kv[:, :, 0, :], preferred_element_type=jnp.float32
        )
        * scaling
    )
    scores = jnp.where(allowed[None, None, :, :], scores, masked_value)
    highest = jnp.max(scores, -1, keepdims=True)
    expo = jnp.exp(scores - highest)
    weights = (expo / jnp.sum(expo, -1, keepdims=True)).astype(jnp.bfloat16)
    train_attention = jnp.einsum(
        "kgts,skd->tkgd", weights, train_kv[:, :, 1, :], preferred_element_type=jnp.float32
    )
    train_attention = train_attention.astype(jnp.bfloat16).reshape(
        train_count, train_queries.shape[1]
    )
    return (decoded, train_attention, handover)


def solution(mesh):
    return jax.shard_map(
        local,
        mesh=mesh,
        in_specs=(
            P("fsdp", None, None),
            P("fsdp", None, "tensor"),
            P("fsdp", None, "tensor"),
            P("fsdp", None),
            P("fsdp"),
            P("fsdp"),
            P("fsdp", None),
            P("fsdp", "tensor"),
            P("fsdp", None),
            P("fsdp", "tensor"),
            P("tensor"),
        ),
        out_specs=(P("fsdp", None, "tensor"), P("fsdp", "tensor"), P("fsdp", None, "tensor")),
        check_vma=False,
    )
```

profile of v0, /device:TPU:1, one launch (start us, length us, event | category | flops | bytes accessed | tf_op | source)
XLA Modules:
  0.0 314.4 jit_solution(10086083105074113274)
XLA Ops:
  7.2 0.7 all-gather.2.cloned.1.call-update
  7.9 0.7 compare_and_fusion
  8.7 0.7 compare_select_fusion
  9.7 0.9 reshape.240
  10.6 1.2 reshape.241
  11.9 2.8 gather_fusion
  14.7 7.0 %gather.8 = bf16[16,512,1,2,128]{4,3,1,0,2:T(2,128)(2,1)} reshape(bf16[128,64,256]{2,1,0:T(8,128)(2,1)} %gather_fusion) | data formatting | bytes 8388608 | tf_op jit(solution)/shard_map/while/body/eval_jaxpr/jit(_take)/gather | solution.py:64
  21.8 3.7 %copy_select_fusion = bf16[16,512,1,2,128]{4,1,0,3,2:T(8,128)(2,1)S(1)} fusion(bf16[16,512,1,2,128]{4,3,1,0,2:T(2,128)(2,1)} %gather.8, pred[16,512]{1,0:T(8,128)(4,1)S(1)} %broadcast_in_dim.95), kind=kLoop, calls=%fused_computation.1 | loop fusion | flops 2097152 | bytes 8396800 | tf_op jit(solution)/shard_map/while/body/eval_jaxpr/jit(_take)/select_n | solution.py:64
  25.5 2.0 copy-done.1
  27.5 0.8 fusion.31
  28.3 227.7 %all-gather.2.cloned.1.call-done = bf16[8192,256]{1,0:T(8,128)(2,1)} async-done(((bf16[64,256]{1,0:T(8,128)(2,1)}), bf16[8192,256]{1,0:T(8,128)(2,1)}) %all-gather.2.cloned.1.call-update) | async-done | bytes 4194320 | tf_op jit(solution)/shard_map/all_gather | solution.py:35
  256.0 3.0 fusion.14
  259.1 3.0 fusion.12
  262.1 0.3 fusion.33
  262.5 0.2 fusion.9
  262.8 0.7 copy.63
  263.7 0.7 reshape.253
  264.4 15.8 %all-to-all-start = ((bf16[128,2,256]{2,1,0:T(2,128)(2,1)}), bf16[128,2,256]{2,1,0:T(2,128)(2,1)S(1)}, u32[]{:S(2)}, u32[]{:S(2)}) async-start(bf16[128,2,256]{2,1,0:T(2,128)(2,1)} %reshape.253), calls=%async_computation | async-start | bytes 262144 | tf_op jit(solution)/shard_map/all_to_all | solution.py:54
  280.2 0.4 fusion.32
  280.7 0.2 fusion.16
  281.2 2.0 fusion.11
  283.3 0.7 reshape.246
  283.9 23.0 %all-to-all-done = bf16[128,2,256]{2,1,0:T(2,128)(2,1)S(1)} async-done(((bf16[128,2,256]{2,1,0:T(2,128)(2,1)}), bf16[128,2,256]{2,1,0:T(2,128)(2,1)S(1)}, u32[]{:S(2)}, u32[]{:S(2)}) %all-to-all-start) | async-done | bytes 131104 | tf_op jit(solution)/shard_map/all_to_all | solution.py:54
  306.9 0.7 copy.65
  (37 shorter events, 1.4 us)
Async XLA Ops:
  7.2 4.7 %copy-start = (bf16[32,64,256]{2,1,0:T(8,128)(2,1)S(1)}, bf16[32,64,256]{2,1,0:T(8,128)(2,1)}, u32[]{:S(2)}) copy-start(bf16[32,64,256]{2,1,0:T(8,128)(2,1)} %param.13) | copy-start | bytes 3145732
  7.2 248.8 %all-gather.2.cloned.1.call-start = ((), (), s32[]{:S(2)}) async-start(), calls=%async_computation.1 | async-start | bytes 4227072 | tf_op jit(solution)/shard_map/all_gather | solution.py:35
  14.7 7.0 %copy-start.7 = (s32[16]{0:T(128)S(1)}, s32[16]{0:T(128)}, u32[]{:S(2)}) copy-start(s32[16]{0:T(128)} %param.15) | copy-start | bytes 196
  14.7 7.1 %copy-start.5 = (s32[1,64]{1,0:T(1,128)S(1)}, s32[1,64]{1,0:T(1,128)}, u32[]{:S(2)}) copy-start(s32[1,64]{1,0:T(1,128)} %param.19) | copy-start | bytes 772
  21.8 234.1 %copy-start.4 = (f32[256]{0:T(256)S(1)}, f32[256]{0:T(256)}, u32[]{:S(2)}) copy-start(f32[256]{0:T(256)} %param.21) | copy-start | bytes 3076
  25.5 2.0 copy-start.1
  27.5 231.6 %copy-start.2 = (bf16[64,8192]{1,0:T(8,128)(2,1)S(1)}, bf16[64,8192]{1,0:T(8,128)(2,1)}, u32[]{:S(2)}) copy-start(bf16[64,8192]{1,0:T(8,128)(2,1)} %param.17) | copy-start | bytes 3145732
  28.3 233.9 %copy-start.3 = (bf16[64,1024]{1,0:T(8,128)(2,1)S(1)}, bf16[64,1024]{1,0:T(8,128)(2,1)}, u32[]{:S(2)}) copy-start(bf16[64,1024]{1,0:T(8,128)(2,1)} %param.18) | copy-start | bytes 393220
  259.0 4.5 %copy-start.6 = (s32[16]{0:T(128)S(1)}, s32[16]{0:T(128)}, u32[]{:S(2)}) copy-start(s32[16]{0:T(128)} %param.16) | copy-start | bytes 196
  264.4 42.5 %all-to-all-start = ((bf16[128,2,256]{2,1,0:T(2,128)(2,1)}), bf16[128,2,256]{2,1,0:T(2,128)(2,1)S(1)}, u32[]{:S(2)}, u32[]{:S(2)}) async-start(bf16[128,2,256]{2,1,0:T(2,128)(2,1)} %reshape.253), calls=%async_computation | async-start | bytes 262144 | tf_op jit(solution)/shard_map/all_to_all | solution.py:54
Sparse Core Ops, SparseCore 0:
  10.7 245.2 all-gather.1
where the time goes:
time: 315 us; the launch traced here: 314 us
  waiting for transfers between devices  251 us (80%)
  local copies, waits for them, and re-layouts  17.2 us (5%)
  starting transfers between devices  15.8 us (5%)
  between operations  14.3 us (5%)
  matrix products  10.1 us (3%)
  other arithmetic  5.62 us (2%)
    all_gather x1, waiting for transfers between devices, local(): gathered = lax.all_gather(project_weight, 'fsdp', axis=0, tiled=True)  228 us
    all_to_all x1, waiting for transfers between devices, local(): lax.all_to_all(outgoing, 'fsdp', split_axis=0, concat_axis=0, tiled=True)  23 us
    all_to_all x1, starting transfers between devices, local(): lax.all_to_all(outgoing, 'fsdp', split_axis=0, concat_axis=0, tiled=True)  15.8 us
    gather x2, local copies, waits for them, and re-layouts, decode_block(): jnp.take(paged_cache, tables, axis=0)  9.75 us
  transfers between devices with their start and end apart: 2, of which 2 were waited for; matrix products, arithmetic and copies ran while one was open for 7% of the time, Pallas kernels for 0%

commit v1 on v0

v1 whole, which is shorter than its diff:
```python
import jax
import jax.numpy as jnp
from jax import lax
from jax.experimental import pallas as pl
from jax.experimental.pallas import tpu as pltpu
from jax.sharding import PartitionSpec as P

HEADS = 64
KV_HEADS = 8
HEAD_DIM = 128
GROUP = HEADS // KV_HEADS
MESH = pl.DeviceIdType.MESH
SCALE = HEAD_DIM ** (-0.5)
MASKED = -1e30

RUNS = 4
PLACES = 4
YS = 4
CORES = 2
ROWS_DEV = 16
TRAIN_DEV = 64
BLOCK = 64
WIDTH = 8192
COLS = 256
PAGE = 64
MAX_PAGES = 8
CONTEXT = PAGE * MAX_PAGES
NEW = ROWS_DEV * 2


def dot_nt(a, b):
    return lax.dot_general(a, b, (((1,), (1,)), ((), ())), preferred_element_type=jnp.float32)


def kernel(
    table_ref,
    length_ref,
    destination_ref,
    documents_ref,
    bias_ref,
    queries_ref,
    train_queries_ref,
    new_hidden_hbm,
    train_hidden_hbm,
    cache_hbm,
    weight_hbm,
    decoded_ref,
    train_out_ref,
    handover_ref,
    wbuf,
    hbuf,
    pool,
    mbuf,
    fbuf,
    acc,
    kvbuf,
    scores,
    hstage,
    hrecv,
    local_sem,
    w_chain_send,
    w_chain_recv,
    w_group_send,
    w_group_recv,
    m_chain_send,
    m_chain_recv,
    m_group_send,
    m_group_recv,
    f_chain_send,
    f_chain_recv,
    f_group_send,
    f_group_recv,
    y_send,
    y_relay_send,
    y_recv,
    p_send,
    p_recv,
    h_send,
    h_recv,
):
    me = lax.axis_index("fsdp")
    core = me % CORES
    y = (me // CORES) % YS
    z = me // (CORES * YS)
    place = z % PLACES
    run = z // PLACES
    y_before = (y + YS - 1) % YS
    y_after = (y + 1) % YS
    y_across = (y + 2) % YS
    other = 1 - core
    octet = y * CORES + core

    def device(zz, yy, cc):
        return (zz * YS + yy) * CORES + cc

    def remote(src, dst, ssem, rsem, target):
        return pltpu.make_async_remote_copy(
            src_ref=src,
            dst_ref=dst,
            send_sem=ssem,
            recv_sem=rsem,
            device_id={"fsdp": target},
            device_id_type=MESH,
        )

    def when(cond, do):
        if cond is True:
            do()
        else:
            pl.when(cond)(do)

    def both(a, b):
        if a is True:
            return b
        if b is True:
            return a
        return jnp.logical_and(a, b)

    pending = []

    def send(cond, make):
        when(cond, lambda: make().start())
        pending.append((cond, make))

    def settle():
        for cond, make in pending:
            when(cond, lambda make=make: make().wait_send())
        pending.clear()

    own_w = wbuf.at[y, run, place, core]
    w_copy = pltpu.make_async_copy(weight_hbm, own_w, local_sem.at[0])
    pool_copy = pltpu.make_async_copy(cache_hbm, pool, local_sem.at[1])
    new_copy = pltpu.make_async_copy(new_hidden_hbm, hbuf.at[pl.ds(0, NEW)], local_sem.at[2])
    train_copy = pltpu.make_async_copy(
        train_hidden_hbm, hbuf.at[pl.ds(NEW, TRAIN_DEV)], local_sem.at[3]
    )
    w_copy.start()
    pool_copy.start()
    new_copy.start()
    train_copy.start()

    lane = lax.broadcasted_iota(jnp.int32, (1, 128), 1)
    wanted = jnp.zeros((1, 128), jnp.float32)
    for r in range(ROWS_DEV):
        value = (destination_ref[r] + 1).astype(jnp.float32)
        hit = (lane // NEW == place) & ((lane % NEW) // 2 == r)
        wanted = jnp.where(hit, value, wanted)
    mbuf[run, place] = wanted

    barrier = pltpu.get_barrier_semaphore()
    for step in range(1, YS * CORES):
        pl.semaphore_signal(
            barrier,
            inc=1,
            device_id={"fsdp": z * (YS * CORES) + (octet + step) % (YS * CORES)},
            device_id_type=MESH,
        )
    expected = jnp.int32(YS * CORES - 1)
    for cond, zz in (
        (run > 0, z - PLACES),
        (run < RUNS - 1, z + PLACES),
        (place > 0, z - 1),
        (place < PLACES - 1, z + 1),
    ):

        @pl.when(cond)
        def _(zz=zz):
            pl.semaphore_signal(
                barrier, inc=1, device_id={"fsdp": device(zz, y, core)}, device_id_type=MESH
            )

        expected = expected + cond.astype(jnp.int32)
    pl.semaphore_wait(barrier, expected)

    class Along:
        def __init__(self, parts):
            self.parts = parts

        def chain_send(self, cond, side, rr, first=False):
            for block, source, cs, cr, _, _ in self.parts:
                src = source if (first and source is not None) else block(rr, place)
                send(
                    cond,
                    lambda src=src, block=block, cs=cs, cr=cr: remote(
                        src,
                        block(rr, place),
                        cs.at[(side + 1) // 2, rr],
                        cr.at[rr],
                        device(z + PLACES * side, y, core),
                    ),
                )

        def chain_wait(self, rr):
            for block, _, cs, cr, _, _ in self.parts:
                remote(
                    block(rr, place), block(rr, place), cs.at[0, rr], cr.at[rr], device(z, y, other)
                ).wait_recv()

        def group_send(self, cond, side, rr, pp, first=False):
            for block, source, _, _, gs, gr in self.parts:
                src = source if (first and source is not None) else block(rr, pp)
                send(
                    cond,
                    lambda src=src, block=block, gs=gs, gr=gr: remote(
                        src,
                        block(rr, pp),
                        gs.at[(side + 1) // 2, rr, pp],
                        gr.at[rr, pp],
                        device(z + side, y, core),
                    ),
                )

        def group_wait(self, rr, pp):
            for block, _, _, _, gs, gr in self.parts:
                remote(
                    block(rr, pp),
                    block(rr, pp),
                    gs.at[0, rr, pp],
                    gr.at[rr, pp],
                    device(z, y, other),
                ).wait_recv()

        def start(self):
            self.chain_send(run < RUNS - 1, 1, run, first=True)
            self.chain_send(run > 0, -1, run, first=True)

        def chain(self, d):
            low, high = run - d, run + d
            when(low >= 0, lambda: self.chain_wait(low))
            self.chain_send(both(low >= 0, run < RUNS - 1), 1, low)
            when(high < RUNS, lambda: self.chain_wait(high))
            self.chain_send(both(high < RUNS, run > 0), -1, high)

        def spread(self, d):
            for cond, rr in quads(d):
                self.group_send(both(cond, place < PLACES - 1), 1, rr, place, first=d == 0)
                self.group_send(both(cond, place > 0), -1, rr, place, first=d == 0)

        def step(self, d, k):
            low, high = place - k, place + k
            for cond, rr in quads(d):
                when(both(cond, low >= 0), lambda rr=rr: self.group_wait(rr, low))
                self.group_send(
                    both(cond, both(low >= 0, place < PLACES - 1)), 1, rr, low
                )
                when(both(cond, high < PLACES), lambda rr=rr: self.group_wait(rr, high))
                self.group_send(both(cond, both(high < PLACES, place > 0)), -1, rr, high)

    def quads(d):
        if d == 0:
            return [(True, run)]
        return [(run - d >= 0, run - d), (run + d < RUNS, run + d)]

    weights = Along(
        [
            (
                lambda rr, pp: wbuf.at[y, rr, pp, core],
                weight_hbm,
                w_chain_send,
                w_chain_recv,
                w_group_send,
                w_group_recv,
            ),
            (
                lambda rr, pp: mbuf.at[rr, pp],
                None,
                m_chain_send,
                m_chain_recv,
                m_group_send,
                m_group_recv,
            ),
        ]
    )

    def quad(yy, rr):
        return wbuf.at[yy, rr, :, core]

    def pass_over(cond, yy, rr):
        send(
            cond,
            lambda: remote(
                quad(yy, rr),
                quad(yy, rr),
                p_send.at[yy, rr],
                p_recv.at[yy, rr],
                device(z, y, other),
            ),
        )

    def y_out(d):
        for cond, rr in quads(d):
            for side, yy in ((0, y_before), (1, y_after)):
                send(
                    cond,
                    lambda rr=rr, side=side, yy=yy: remote(
                        quad(y, rr),
                        quad(y, rr),
                        y_send.at[side, rr],
                        y_recv.at[y, rr],
                        device(z, yy, core),
                    ),
                )
            pass_over(cond, y, rr)

    def y_wait(yy, rr):
        remote(
            quad(yy, rr), quad(yy, rr), y_send.at[0, rr], y_recv.at[yy, rr], device(z, y, other)
        ).wait_recv()

    def y_in(d):
        source = jnp.where(core == 0, y_before, y_after)
        target = jnp.where(core == 0, y_after, y_before)
        for cond, rr in quads(d):
            when(cond, lambda rr=rr: y_wait(source, rr))
            send(
                cond,
                lambda rr=rr: remote(
                    quad(source, rr),
                    quad(source, rr),
                    y_relay_send.at[rr],
                    y_recv.at[source, rr],
                    device(z, target, core),
                ),
            )
            pass_over(cond, source, rr)
            when(cond, lambda rr=rr: y_wait(target, rr))
            pass_over(cond, target, rr)

    def y_last(d):
        for cond, rr in quads(d):
            when(cond, lambda rr=rr: y_wait(y_across, rr))
            pass_over(cond, y_across, rr)

    def partner_wait(yy, rr):
        landed = wbuf.at[yy, rr, :, other]
        remote(
            landed, landed, p_send.at[yy, rr], p_recv.at[yy, rr], device(z, y, other)
        ).wait_recv()

    def multiply(yy, rr):
        partner_wait(yy, rr)
        parts = []
        for pp in range(PLACES):
            start = ((rr * PLACES + pp) * YS + yy) * (CORES * BLOCK)
            parts.append(hbuf[:, pl.ds(pl.multiple_of(start, 128), CORES * BLOCK)])
        left = jnp.concatenate(parts, axis=1)
        right = wbuf[yy, rr].reshape(PLACES * CORES * BLOCK, COLS)
        acc[...] += jnp.dot(left, right, preferred_element_type=jnp.float32)

    def multiply_near(d):
        for cond, rr in quads(d):

            def do(rr=rr):
                for yy in (y, y_before, y_after):
                    multiply(yy, rr)

            when(cond, do)

    def multiply_far(d):
        for cond, rr in quads(d):
            when(cond, lambda rr=rr: multiply(y_across, rr))

    position = lax.broadcasted_iota(jnp.int32, (1, CONTEXT), 1)

    def old_scores(rows):
        for r in rows:
            keys = jnp.concatenate(
                [pool[table_ref[r, p], :, 0:HEAD_DIM] for p in range(MAX_PAGES)], axis=0
            )
            values = dot_nt(queries_ref[r], keys) * SCALE
            scores[r] = jnp.where(position < length_ref[r], values, MASKED)

    acc[...] = jnp.zeros_like(acc)
    weights.start()
    weights.spread(0)
    pool_copy.wait()
    old_scores(range(0, 2))
    weights.step(0, 1)
    old_scores(range(2, 4))
    weights.step(0, 2)
    weights.chain(1)
    weights.spread(1)
    weights.step(0, 3)
    w_copy.wait()
    y_out(0)
    old_scores(range(4, 6))
    weights.step(1, 1)
    old_scores(range(6, 8))
    weights.step(1, 2)
    weights.chain(2)
    weights.spread(2)
    weights.step(1, 3)
    y_out(1)
    y_in(0)
    old_scores(range(8, 10))
    weights.step(2, 1)
    old_scores(range(10, 12))
    weights.step(2, 2)
    weights.chain(3)
    weights.spread(3)
    weights.step(2, 3)
    y_out(2)
    y_in(1)
    y_last(0)
    old_scores(range(12, 14))
    weights.step(3, 1)
    old_scores(range(14, 16))
    weights.step(3, 2)
    weights.step(3, 3)
    y_out(3)
    new_copy.wait()
    train_copy.wait()
    multiply_near(0)
    y_in(2)
    y_last(1)
    multiply_far(0)
    multiply_near(1)
    y_in(3)
    y_last(2)
    multiply_far(1)
    multiply_near(2)
    y_last(3)
    multiply_far(2)
    multiply_near(3)
    multiply_far(3)

    fresh = (acc[...] + bias_ref[...]).astype(jnp.bfloat16)
    fbuf[run, place] = fresh[0:NEW]
    kvbuf[...] = fresh

    rows_z = Along(
        [
            (
                lambda rr, pp: fbuf.at[rr, pp],
                None,
                f_chain_send,
                f_chain_recv,
                f_group_send,
                f_group_recv,
            )
        ]
    )

    new_column = lax.broadcasted_iota(jnp.int32, (CORES * GROUP, NEW), 1)
    new_token = lax.broadcasted_iota(jnp.int32, (CORES * GROUP, NEW), 0) // GROUP

    def decode(rows):
        for r in rows:
            values = jnp.concatenate(
                [pool[table_ref[r, p], :, HEAD_DIM : 2 * HEAD_DIM] for p in range(MAX_PAGES)],
                axis=0,
            )
            old = scores[r]
            new = dot_nt(queries_ref[r], kvbuf[0:NEW, 0:HEAD_DIM]) * SCALE
            allowed = (new_column // 2 == r) & (new_column % 2 <= new_token)
            new = jnp.where(allowed, new, MASKED)
            highest = jnp.maximum(
                jnp.max(old, axis=1, keepdims=True), jnp.max(new, axis=1, keepdims=True)
            )
            old = jnp.exp(old - highest)
            new = jnp.exp(new - highest)
            total = jnp.sum(old, axis=1, keepdims=True) + jnp.sum(new, axis=1, keepdims=True)
            inverse = 1.0 / total
            result = jnp.dot(
                (old * inverse).astype(jnp.bfloat16), values, preferred_element_type=jnp.float32
            )
            result = result + jnp.dot(
                (new * inverse).astype(jnp.bfloat16),
                kvbuf[0:NEW, HEAD_DIM : 2 * HEAD_DIM],
                preferred_element_type=jnp.float32,
            )
            decoded_ref[r] = result.astype(jnp.bfloat16)

    doc_row = jnp.broadcast_to(documents_ref[...], (TRAIN_DEV, TRAIN_DEV))
    row_id = lax.broadcasted_iota(jnp.int32, (TRAIN_DEV, TRAIN_DEV), 0)
    col_id = lax.broadcasted_iota(jnp.int32, (TRAIN_DEV, TRAIN_DEV), 1)
    doc_col = jnp.sum(jnp.where(row_id == col_id, doc_row, 0), axis=1, keepdims=True)
    train_mask = (col_id <= row_id) & (doc_row == doc_col)

    def train(heads):
        for g in heads:
            span = slice(g * HEAD_DIM, (g + 1) * HEAD_DIM)
            values = dot_nt(train_queries_ref[:, span], kvbuf[NEW:, 0:HEAD_DIM]) * SCALE
            values = jnp.where(train_mask, values, MASKED)
            expo = jnp.exp(values - jnp.max(values, axis=1, keepdims=True))
            inverse = 1.0 / jnp.sum(expo, axis=1, keepdims=True)
            result = jnp.dot(
                (expo * inverse).astype(jnp.bfloat16),
                kvbuf[NEW:, HEAD_DIM : 2 * HEAD_DIM],
                preferred_element_type=jnp.float32,
            )
            train_out_ref[:, span] = result.astype(jnp.bfloat16)

    rows_z.start()
    rows_z.spread(0)
    decode(range(0, 2))
    rows_z.step(0, 1)
    decode(range(2, 4))
    rows_z.step(0, 2)
    rows_z.chain(1)
    rows_z.spread(1)
    rows_z.step(0, 3)
    decode(range(4, 6))
    rows_z.step(1, 1)
    decode(range(6, 8))
    rows_z.step(1, 2)
    rows_z.chain(2)
    rows_z.spread(2)
    rows_z.step(1, 3)
    decode(range(8, 10))
    rows_z.step(2, 1)
    decode(range(10, 12))
    rows_z.step(2, 2)
    rows_z.chain(3)
    rows_z.spread(3)
    rows_z.step(2, 3)
    decode(range(12, 16))
    rows_z.step(3, 1)
    train(range(0, 4))
    rows_z.step(3, 2)
    train(range(4, 8))
    rows_z.step(3, 3)

    out_row = lax.broadcasted_iota(jnp.int32, (64, 128), 0)
    in_row = lax.broadcasted_iota(jnp.int32, (64, 128), 1)
    owner = (z * (YS * CORES) + out_row // 8 + 1).astype(jnp.float32)
    same = ((out_row // 2) % PLACES == in_row // NEW) & (out_row % 2 == in_row % 2)
    pieces = []
    for rr in range(RUNS):
        asked = mbuf[rr, 0] + mbuf[rr, 1] + mbuf[rr, 2] + mbuf[rr, 3]
        chosen = jnp.where(same & (asked == owner), 1.0, 0.0).astype(jnp.bfloat16)
        rows = fbuf[rr].reshape(PLACES * NEW, COLS)
        pieces.append(jnp.dot(chosen, rows, preferred_element_type=jnp.float32))
    for o in range(YS * CORES):
        rows = jnp.concatenate([piece[o * 8 : (o + 1) * 8] for piece in pieces], axis=0)
        hstage[o] = rows.astype(jnp.bfloat16)
    for step in range(1, YS * CORES):
        target = (octet + step) % (YS * CORES)
        send(
            True,
            lambda step=step, target=target: remote(
                hstage.at[target],
                hrecv.at[octet],
                h_send.at[step],
                h_recv.at[octet],
                z * (YS * CORES) + target,
            ),
        )
    hrecv[octet] = hstage[octet]
    settle()
    for step in range(1, YS * CORES):
        source = (octet + step) % (YS * CORES)
        remote(
            hstage.at[source],
            hrecv.at[source],
            h_send.at[step],
            h_recv.at[source],
            z * (YS * CORES) + source,
        ).wait_recv()
    handover_ref[...] = hrecv[...]


def local(
    new_hidden,
    new_queries,
    paged_cache,
    block_table,
    lengths,
    destination,
    train_hidden,
    train_queries,
    documents,
    project_weight,
    project_bias,
):
    vmem = pl.BlockSpec(memory_space=pltpu.VMEM)
    smem = pl.BlockSpec(memory_space=pltpu.SMEM)
    anywhere = pl.BlockSpec(memory_space=pl.ANY)
    dma = pltpu.SemaphoreType.DMA
    along = [dma((2, RUNS)), dma((RUNS,)), dma((2, RUNS, PLACES)), dma((RUNS, PLACES))]
    decoded, attended, handed = pl.pallas_call(
        kernel,
        out_shape=(
            jax.ShapeDtypeStruct((ROWS_DEV, CORES * GROUP, HEAD_DIM), jnp.bfloat16),
            jax.ShapeDtypeStruct((TRAIN_DEV, GROUP * HEAD_DIM), jnp.bfloat16),
            jax.ShapeDtypeStruct((YS * CORES, RUNS * PLACES * 2, COLS), jnp.bfloat16),
        ),
        in_specs=[smem, smem, smem, vmem, vmem, vmem, vmem] + [anywhere] * 4,
        out_specs=(vmem, vmem, vmem),
        scratch_shapes=[
            pltpu.VMEM((YS, RUNS, PLACES, CORES, BLOCK, COLS), jnp.bfloat16),
            pltpu.VMEM((NEW + TRAIN_DEV, WIDTH), jnp.bfloat16),
            pltpu.VMEM((paged_cache.shape[0], PAGE, COLS), jnp.bfloat16),
            pltpu.VMEM((RUNS, PLACES, 1, 128), jnp.float32),
            pltpu.VMEM((RUNS, PLACES, NEW, COLS), jnp.bfloat16),
            pltpu.VMEM((NEW + TRAIN_DEV, COLS), jnp.float32),
            pltpu.VMEM((NEW + TRAIN_DEV, COLS), jnp.bfloat16),
            pltpu.VMEM((ROWS_DEV, CORES * GROUP, CONTEXT), jnp.float32),
            pltpu.VMEM((YS * CORES, RUNS * PLACES * 2, COLS), jnp.bfloat16),
            pltpu.VMEM((YS * CORES, RUNS * PLACES * 2, COLS), jnp.bfloat16),
            dma((4,)),
            *along,
            *along,
            *along,
            dma((2, RUNS)),
            dma((RUNS,)),
            dma((YS, RUNS)),
            dma((YS, RUNS)),
            dma((YS, RUNS)),
            dma((YS * CORES,)),
            dma((YS * CORES,)),
        ],
        compiler_params=pltpu.CompilerParams(collective_id=0, has_side_effects=True),
    )(
        block_table,
        lengths,
        destination,
        documents,
        project_bias.reshape(1, COLS),
        new_queries.reshape(ROWS_DEV, 2 * GROUP, HEAD_DIM),
        train_queries,
        new_hidden.reshape(NEW, WIDTH),
        train_hidden,
        paged_cache,
        project_weight,
    )
    decoded = decoded.reshape(ROWS_DEV, 2, GROUP * HEAD_DIM)
    handed = handed.reshape(YS * CORES, RUNS * PLACES, 2, COLS).transpose(1, 0, 2, 3)
    return decoded, attended, handed.reshape(RUNS * PLACES * YS * CORES, 2, COLS)


def solution(mesh):
    return jax.shard_map(
        local,
        mesh=mesh,
        in_specs=(
            P("fsdp", None, None),
            P("fsdp", None, "tensor"),
            P("fsdp", None, "tensor"),
            P("fsdp", None),
            P("fsdp"),
            P("fsdp"),
            P("fsdp", None),
            P("fsdp", "tensor"),
            P("fsdp", None),
            P("fsdp", "tensor"),
            P("tensor"),
        ),
        out_specs=(P("fsdp", None, "tensor"), P("fsdp", "tensor"), P("fsdp", None, "tensor")),
        check_vma=False,
    )
```

time: 315 us -> 101 us (0.32)
  waiting for transfers between devices: 251 us -> 0 us
  Pallas kernels: 0 us -> 91.9 us
  starting transfers between devices: 15.8 us -> 0 us
  between operations: 14.3 us -> 0.66 us
  matrix products: 10.1 us -> 0 us
  local copies, waits for them, and re-layouts: 17.2 us -> 8.04 us
  other arithmetic: 5.62 us -> 0 us
    all_gather x1 -> x0, waiting for transfers between devices: 228 us -> none  [local(): gathered = lax.all_gather(project_weight, 'fsdp', axis=0, tiled=True)]
    pallas_call x0 -> x1, Pallas kernels: none -> 91.9 us  [local(): pl.pallas_call(kernel, out_shape=(jax.ShapeDtypeStruct((ROWS_DEV, CORES *...]
    all_to_all x1 -> x0, waiting for transfers between devices: 23 us -> none  [local(): lax.all_to_all(outgoing, 'fsdp', split_axis=0, concat_axis=0, tiled=True)]
    all_to_all x1 -> x0, starting transfers between devices: 15.8 us -> none  [local(): lax.all_to_all(outgoing, 'fsdp', split_axis=0, concat_axis=0, tiled=True)]
    dot_general x9 -> x0, matrix products: 10.1 us -> none  [the longest x1 3.01 us: local(): decode_sum = jnp.dot(flat_new, gathered, preferred_element_type=jnp.float32)]
    gather x2 -> x0, local copies, waits for them, and re-layouts: 9.75 us -> none  [decode_block(): jnp.take(paged_cache, tables, axis=0)]
    select_n x2 -> x0, other arithmetic: 4.36 us -> none  [decode_block(): jnp.take(paged_cache, tables, axis=0)]
  transfers between devices with their start and end apart: 2 -> 0, of which waited for: 2 -> 0; matrix products, arithmetic and copies ran while one was open for 7% -> 0% of each run, Pallas kernels for 0% -> 0%
where the time goes in v1:
time: 101 us
  Pallas kernels  91.9 us (91%)
  local copies, waits for them, and re-layouts  8.04 us (8%)
    pallas_call x1, Pallas kernels, local(): pl.pallas_call(kernel, out_shape=(jax.ShapeDtypeStruct((ROWS_DEV, CORES *...  91.9 us
    unnamed x6, local copies, waits for them, and re-layouts  2.16 us
    reshape x1, local copies, waits for them, and re-layouts, local(): new_hidden.reshape(NEW, WIDTH)  2.03 us

profile of v1, /device:TPU:1, one launch (start us, length us, event | category | flops | bytes accessed | tf_op | source)
XLA Modules:
  0.0 100.6 jit_solution(14926077986396584168)
XLA Ops:
  0.6 1.4 %copy.14.table_ref = s32[16,8]{1,0:T(8,128)} copy(s32[16,8]{0,1:T(8,128)} %param.14) | data formatting | bytes 1024 | tf_op args[3]
  2.0 1.5 %reshape.25.queries_ref = bf16[16,16,128]{2,1,0:T(8,128)(2,1)} reshape(bf16[16,2,1024]{2,1,0:T(2,128)(2,1)} %param.12) | data formatting | bytes 131072 | tf_op jit(solution)/shard_map/reshape | solution.py:620
  3.5 2.0 %reshape.26.new_hidden_hbm = bf16[32,8192]{1,0:T(8,128)(2,1)} reshape(bf16[16,2,8192]{2,1,0:T(2,128)(2,1)} %param.11) | data formatting | bytes 1048576 | tf_op jit(solution)/shard_map/reshape | solution.py:622
  5.5 91.9 %shard_map.130 = (bf16[16,16,128]{2,1,0:T(8,128)(2,1)}, bf16[64,1024]{1,0:T(8,128)(2,1)}, bf16[8,32,256]{2,1,0:T(8,128)(2,1)}) custom-call(s32[16,8]{1,0:T(8,128)} %copy.14.table_ref, s32[16]{0:T(128)} %length_ref.1, s32[16]{0:T(128)} %destination_ref.1, s32[1,64]{1,0:T(1,128)} %documents_ref.1, f32[1,256]{1,0:T(1,128)} %bitcast.5, ...), custom_call_target="tpu_custom_call" | custom-call | tf_op jit(solution)/shard_map/pallas_call | solution.py:581
  97.5 0.0 copy-start.1
  97.5 1.5 %reshape.27 = bf16[16,2,1024]{2,1,0:T(2,128)(2,1)} reshape(bf16[16,16,128]{2,1,0:T(8,128)(2,1)} %get-tuple-element.6) | data formatting | bytes 131072 | tf_op jit(solution)/shard_map/reshape | solution.py:627
  99.0 0.0 copy-done.1
  99.0 0.1 reshape.28
  99.1 0.0 copy-start
  99.1 0.7 copy.15
  99.8 0.1 copy-done
  100.0 0.7 copy.17
Async XLA Ops:
  97.5 1.5 %copy-start.1 = (bf16[8,32,256]{2,1,0:T(8,128)(2,1)S(1)}, bf16[8,32,256]{2,1,0:T(8,128)(2,1)}, u32[]{:S(2)}) copy-start(bf16[8,32,256]{2,1,0:T(8,128)(2,1)} %get-tuple-element.8) | copy-start | bytes 393220
  99.1 0.9 copy-start

commit v2 on v1

v2 whole, which is shorter than its diff:
```python
import jax
import jax.numpy as jnp
from jax import lax
from jax.experimental import pallas as pl
from jax.experimental.pallas import tpu as pltpu
from jax.sharding import PartitionSpec as P

HEADS = 64
KV_HEADS = 8
HEAD_DIM = 128
GROUP = HEADS // KV_HEADS
MESH = pl.DeviceIdType.MESH
SCALE = HEAD_DIM ** (-0.5)
MASKED = -1e30

RUNS = 4
PLACES = 4
YS = 4
CORES = 2
ROWS_DEV = 16
TRAIN_DEV = 64
BLOCK = 64
WIDTH = 8192
COLS = 256
PAGE = 64
MAX_PAGES = 8
CONTEXT = PAGE * MAX_PAGES
NEW = ROWS_DEV * 2
ALL_ROWS = NEW + TRAIN_DEV
LANES = CORES * BLOCK
RELAY_CHAIN = False
RELAY_GROUP = True


def dot_nt(a, b):
    return lax.dot_general(a, b, (((1,), (1,)), ((), ())), preferred_element_type=jnp.float32)


def kernel(
    table_ref,
    length_ref,
    destination_ref,
    documents_ref,
    bias_ref,
    queries_ref,
    train_queries_ref,
    new_hidden_hbm,
    train_hidden_hbm,
    cache_hbm,
    weight_hbm,
    decoded_ref,
    train_out_ref,
    handover_ref,
    wbuf,
    hbuf,
    raw,
    qbuf,
    pool,
    mbuf,
    fbuf,
    gbuf,
    acc,
    rbuf,
    kvbuf,
    scores,
    hstage,
    hrecv,
    local_sem,
    w_chain_send,
    w_chain_recv,
    w_group_send,
    w_group_recv,
    m_chain_send,
    m_chain_recv,
    m_group_send,
    m_group_recv,
    f_chain_send,
    f_chain_recv,
    f_group_send,
    f_group_recv,
    relay_send,
    own_sem,
    y_send,
    y_recv,
    r_send,
    r_recv,
    p_send,
    p_recv,
    h_send,
    h_recv,
):
    me = lax.axis_index("fsdp")
    core = me % CORES
    y = (me // CORES) % YS
    z = me // (CORES * YS)
    place = z % PLACES
    run = z // PLACES
    other = 1 - core
    octet = y * CORES + core

    def device(zz, yy, cc):
        return (zz * YS + yy) * CORES + cc

    def remote(src, dst, ssem, rsem, target):
        return pltpu.make_async_remote_copy(
            src_ref=src,
            dst_ref=dst,
            send_sem=ssem,
            recv_sem=rsem,
            device_id={"fsdp": target},
            device_id_type=MESH,
        )

    def when(cond, do):
        if cond is True:
            do()
        else:
            pl.when(cond)(do)

    def both(a, b):
        if a is True:
            return b
        if b is True:
            return a
        return jnp.logical_and(a, b)

    pending = []

    def send(cond, make):
        when(cond, lambda: make().start())
        pending.append((cond, make))

    def settle():
        for cond, make in pending:
            when(cond, lambda make=make: make().wait_send())
        pending.clear()

    own_w = wbuf.at[run, place, core]
    w_copy = pltpu.make_async_copy(weight_hbm, own_w, local_sem.at[0])
    pool_copy = pltpu.make_async_copy(cache_hbm, pool, local_sem.at[1])
    new_copy = pltpu.make_async_copy(new_hidden_hbm, raw, local_sem.at[2])
    train_copy = pltpu.make_async_copy(
        train_hidden_hbm, hbuf.at[pl.ds(NEW, TRAIN_DEV)], local_sem.at[3]
    )
    w_copy.start()
    pool_copy.start()
    new_copy.start()
    train_copy.start()

    lane = lax.broadcasted_iota(jnp.int32, (1, 128), 1)
    wanted = jnp.zeros((1, 128), jnp.float32)
    for r in range(ROWS_DEV):
        value = (destination_ref[r] + 1).astype(jnp.float32)
        hit = (lane // NEW == place) & ((lane % NEW) // 2 == r)
        wanted = jnp.where(hit, value, wanted)
    mbuf[run, place] = wanted

    barrier = pltpu.get_barrier_semaphore()
    for step in range(1, YS * CORES):
        pl.semaphore_signal(
            barrier,
            inc=1,
            device_id={"fsdp": z * (YS * CORES) + (octet + step) % (YS * CORES)},
            device_id_type=MESH,
        )
    expected = jnp.int32(YS * CORES - 1)
    near = [
        (jnp.logical_and(run + side * far >= 0, run + side * far < RUNS), z + side * far * PLACES)
        for far in (1, 2, 3)
        for side in (1, -1)
    ] + [
        (jnp.logical_and(place + side * far >= 0, place + side * far < PLACES), z + side * far)
        for far in (1, 2, 3)
        for side in (1, -1)
    ]
    for cond, zz in near:

        @pl.when(cond)
        def _(zz=zz):
            pl.semaphore_signal(
                barrier, inc=1, device_id={"fsdp": device(zz, y, core)}, device_id_type=MESH
            )

        expected = expected + cond.astype(jnp.int32)
    for r in range(ROWS_DEV):
        both_tokens = queries_ref[r]
        qbuf[r] = jnp.concatenate(
            [both_tokens[:, g * HEAD_DIM : (g + 1) * HEAD_DIM] for g in range(GROUP)], axis=0
        )
    new_copy.wait()
    hbuf[0:NEW] = raw[...].reshape(NEW, WIDTH)
    pl.semaphore_wait(barrier, expected)

    class Along:
        def __init__(self, parts, relay=None):
            self.parts = parts
            self.relay = relay

        def start(self):
            for far in (2, 1) if self.relay is not None and RELAY_CHAIN else (3, 2, 1):
                for side in (1, -1):
                    target = run + side * far
                    cond = jnp.logical_and(target >= 0, target < RUNS)
                    for block, source, cs, cr, _, _ in self.parts:
                        src = block(run, place) if source is None else source
                        send(
                            cond,
                            lambda src=src, block=block, cs=cs, cr=cr, target=target: remote(
                                src,
                                block(run, place),
                                cs.at[target],
                                cr.at[run],
                                device(target * PLACES + place, y, core),
                            ),
                        )

        def chain(self, d):
            for cond, rr in quads(d):

                def do(rr=rr):
                    for block, _, cs, cr, _, _ in self.parts:
                        remote(
                            block(rr, place),
                            block(rr, place),
                            cs.at[rr],
                            cr.at[rr],
                            device(z, y, other),
                        ).wait_recv()

                when(cond, do)
                if d == 2 and self.relay is not None and RELAY_CHAIN:
                    onward = run + jnp.where(rr < run, 1, -1)
                    ahead = both(cond, jnp.logical_and(onward >= 0, onward < RUNS))
                    for i, (block, _, cs, cr, _, _) in enumerate(self.parts):
                        send(
                            ahead,
                            lambda rr=rr, i=i, block=block, cr=cr, onward=onward: remote(
                                block(rr, place),
                                block(rr, place),
                                self.relay.at[i, RUNS],
                                cr.at[rr],
                                device(onward * PLACES + place, y, core),
                            ),
                        )

        def spread(self, d):
            for cond, rr in quads(d):
                for far in (2, 1) if self.relay is not None and RELAY_GROUP else (3, 2, 1):
                    for side in (1, -1):
                        target = place + side * far
                        inside = both(cond, jnp.logical_and(target >= 0, target < PLACES))
                        for block, source, _, _, gs, gr in self.parts:
                            src = source if (d == 0 and source is not None) else block(rr, place)
                            send(
                                inside,
                                lambda src=src, block=block, gs=gs, gr=gr, rr=rr, target=target: (
                                    remote(
                                        src,
                                        block(rr, place),
                                        gs.at[rr, target],
                                        gr.at[rr, place],
                                        device(run * PLACES + target, y, core),
                                    )
                                ),
                            )

        def gather(self, d):
            for far in (2, 1, 3):
                for side in (1, -1):
                    pp = place + side * far
                    for cond, rr in quads(d):
                        inside = both(cond, jnp.logical_and(pp >= 0, pp < PLACES))

                        def do(rr=rr, pp=pp):
                            for block, _, _, _, gs, gr in self.parts:
                                remote(
                                    block(rr, pp),
                                    block(rr, pp),
                                    gs.at[rr, pp],
                                    gr.at[rr, pp],
                                    device(z, y, other),
                                ).wait_recv()

                        when(inside, do)
                        if far == 2 and self.relay is not None and RELAY_GROUP:
                            onward = place - side
                            ahead = both(
                                inside, jnp.logical_and(onward >= 0, onward < PLACES)
                            )
                            for i, (block, _, _, _, _, gr) in enumerate(self.parts):
                                send(
                                    ahead,
                                    lambda rr=rr, pp=pp, i=i, block=block, gr=gr, onward=onward: (
                                        remote(
                                            block(rr, pp),
                                            block(rr, pp),
                                            self.relay.at[i, rr],
                                            gr.at[rr, pp],
                                            device(run * PLACES + onward, y, core),
                                        )
                                    ),
                                )

    def quads(d):
        if d == 0:
            return [(True, run)]
        return [(run - d >= 0, run - d), (run + d < RUNS, run + d)]

    weights = Along(
        [
            (
                lambda rr, pp: wbuf.at[rr, pp, core],
                weight_hbm,
                w_chain_send,
                w_chain_recv,
                w_group_send,
                w_group_recv,
            ),
            (
                lambda rr, pp: mbuf.at[rr, pp],
                None,
                m_chain_send,
                m_chain_recv,
                m_group_send,
                m_group_recv,
            ),
        ],
        relay_send,
    )

    def pass_over(cond, rr):
        send(
            cond,
            lambda: remote(
                wbuf.at[rr, :, core],
                wbuf.at[rr, :, core],
                p_send.at[rr],
                p_recv.at[rr],
                device(z, y, other),
            ),
        )

    def chained(d):
        weights.chain(d)
        weights.spread(d)

    def gathered(d):
        weights.gather(d)
        for cond, rr in quads(d):
            pass_over(cond, rr)

    def columns(rr, pp, yy):
        start = ((rr * PLACES + pp) * YS + yy) * LANES
        return hbuf.at[:, pl.ds(pl.multiple_of(start, LANES), LANES)]

    def hidden_slot(rr, pp, yy):
        return gbuf.at[rr, yy, :, pl.ds(pp * LANES, LANES)]

    def own_copy(rr, pp):
        return pltpu.make_async_copy(
            columns(rr, pp, y), hidden_slot(rr, pp, y), own_sem.at[rr, pp]
        )

    def hidden_out():
        for rr in range(RUNS):
            for turn in (2, 1, 3):
                yy = (y + turn) % YS
                for pp in range(PLACES):
                    send(
                        True,
                        lambda rr=rr, pp=pp, turn=turn, yy=yy: remote(
                            columns(rr, pp, yy),
                            hidden_slot(rr, pp, y),
                            y_send.at[turn, rr, pp],
                            y_recv.at[y, rr, pp],
                            device(z, yy, core),
                        ),
                    )
            for pp in range(PLACES):
                own_copy(rr, pp).start()

    def hidden_in():
        for rr in range(RUNS):
            for pp in range(PLACES):
                own_copy(rr, pp).wait()
                for turn in (1, 3, 2):
                    yy = (y + turn) % YS
                    landed = hidden_slot(rr, pp, yy)
                    remote(
                        landed,
                        landed,
                        y_send.at[turn, rr, pp],
                        y_recv.at[yy, rr, pp],
                        device(z, y, other),
                    ).wait_recv()

    def multiply(rr):
        landed = wbuf.at[rr, :, other]
        remote(landed, landed, p_send.at[rr], p_recv.at[rr], device(z, y, other)).wait_recv()
        left = gbuf[rr].reshape(YS * ALL_ROWS, PLACES * LANES)
        right = wbuf[rr].reshape(PLACES * LANES, COLS)
        product = jnp.dot(left, right, preferred_element_type=jnp.float32)
        acc[...] += product.reshape(YS, ALL_ROWS, COLS)

    def multiplied(d):
        for cond, rr in quads(d):
            when(cond, lambda rr=rr: multiply(rr))

    def share_rows(part):
        return pl.ds(0, NEW) if part == 0 else pl.ds(NEW, TRAIN_DEV)

    def shares_out(part):
        for turn in (2, 1, 3):
            yy = (y + turn) % YS
            send(
                True,
                lambda turn=turn, yy=yy: remote(
                    acc.at[yy, share_rows(part)],
                    rbuf.at[y, share_rows(part)],
                    r_send.at[part, turn],
                    r_recv.at[part, y],
                    device(z, yy, core),
                ),
            )

    def shares_in(part):
        total = acc[y, share_rows(part)] + bias_ref[...]
        for turn in (1, 3, 2):
            yy = (y + turn) % YS
            landed = rbuf.at[yy, share_rows(part)]
            remote(
                landed, landed, r_send.at[part, turn], r_recv.at[part, yy], device(z, y, other)
            ).wait_recv()
            total = total + rbuf[yy, share_rows(part)]
        return total.astype(jnp.bfloat16)

    position = lax.broadcasted_iota(jnp.int32, (1, CONTEXT), 1)

    def old_scores(rows):
        for r in rows:
            keys = jnp.concatenate(
                [pool[table_ref[p, r], :, 0:HEAD_DIM] for p in range(MAX_PAGES)], axis=0
            )
            values = dot_nt(qbuf[r], keys) * SCALE
            scores[r] = jnp.where(position < length_ref[r], values, MASKED)

    acc[...] = jnp.zeros_like(acc)
    weights.start()
    weights.spread(0)
    train_copy.wait()
    hidden_out()
    pool_copy.wait()
    old_scores(range(0, 16))
    w_copy.wait()
    chained(1)
    chained(2)
    gathered(0)
    chained(3)
    gathered(1)
    gathered(2)
    gathered(3)
    hidden_in()
    multiplied(0)
    multiplied(1)
    multiplied(2)
    multiplied(3)
    shares_out(0)
    fresh = shares_in(0)
    fbuf[run, place] = fresh
    kvbuf[0:NEW] = fresh

    rows_z = Along(
        [
            (
                lambda rr, pp: fbuf.at[rr, pp],
                None,
                f_chain_send,
                f_chain_recv,
                f_group_send,
                f_group_recv,
            )
        ]
    )

    new_column = lax.broadcasted_iota(jnp.int32, (CORES * GROUP, NEW), 1)
    new_token = lax.broadcasted_iota(jnp.int32, (CORES * GROUP, NEW), 0) % 2

    def decode(rows):
        for r in rows:
            values = jnp.concatenate(
                [pool[table_ref[p, r], :, HEAD_DIM : 2 * HEAD_DIM] for p in range(MAX_PAGES)],
                axis=0,
            )
            old = scores[r]
            new = dot_nt(qbuf[r], kvbuf[0:NEW, 0:HEAD_DIM]) * SCALE
            allowed = (new_column // 2 == r) & (new_column % 2 <= new_token)
            new = jnp.where(allowed, new, MASKED)
            highest = jnp.maximum(
                jnp.max(old, axis=1, keepdims=True), jnp.max(new, axis=1, keepdims=True)
            )
            old = jnp.exp(old - highest)
            new = jnp.exp(new - highest)
            total = jnp.sum(old, axis=1, keepdims=True) + jnp.sum(new, axis=1, keepdims=True)
            inverse = 1.0 / total
            result = jnp.dot(
                (old * inverse).astype(jnp.bfloat16), values, preferred_element_type=jnp.float32
            )
            result = result + jnp.dot(
                (new * inverse).astype(jnp.bfloat16),
                kvbuf[0:NEW, HEAD_DIM : 2 * HEAD_DIM],
                preferred_element_type=jnp.float32,
            )
            decoded_ref[r] = jnp.concatenate(
                [result[2 * g : 2 * g + 2] for g in range(GROUP)], axis=1
            ).astype(jnp.bfloat16)

    doc_row = jnp.broadcast_to(documents_ref[...], (TRAIN_DEV, TRAIN_DEV))
    row_id = lax.broadcasted_iota(jnp.int32, (TRAIN_DEV, TRAIN_DEV), 0)
    col_id = lax.broadcasted_iota(jnp.int32, (TRAIN_DEV, TRAIN_DEV), 1)
    doc_col = jnp.sum(jnp.where(row_id == col_id, doc_row, 0), axis=1, keepdims=True)
    train_mask = (col_id <= row_id) & (doc_row == doc_col)

    def train(heads):
        for g in heads:
            span = slice(g * HEAD_DIM, (g + 1) * HEAD_DIM)
            values = dot_nt(train_queries_ref[:, span], kvbuf[NEW:, 0:HEAD_DIM]) * SCALE
            values = jnp.where(train_mask, values, MASKED)
            expo = jnp.exp(values - jnp.max(values, axis=1, keepdims=True))
            inverse = 1.0 / jnp.sum(expo, axis=1, keepdims=True)
            result = jnp.dot(
                (expo * inverse).astype(jnp.bfloat16),
                kvbuf[NEW:, HEAD_DIM : 2 * HEAD_DIM],
                preferred_element_type=jnp.float32,
            )
            train_out_ref[:, span] = result.astype(jnp.bfloat16)

    rows_z.start()
    rows_z.spread(0)
    shares_out(1)
    decode(range(0, 8))
    rows_z.chain(1)
    rows_z.spread(1)
    decode(range(8, 14))
    rows_z.chain(2)
    rows_z.spread(2)
    decode(range(14, 16))
    kvbuf[NEW:] = shares_in(1)
    train(range(0, 4))
    rows_z.chain(3)
    rows_z.spread(3)
    train(range(4, 8))
    rows_z.gather(0)
    rows_z.gather(1)
    rows_z.gather(2)
    rows_z.gather(3)

    out_row = lax.broadcasted_iota(jnp.int32, (64, 128), 0)
    in_row = lax.broadcasted_iota(jnp.int32, (64, 128), 1)
    owner = (z * (YS * CORES) + out_row // 8 + 1).astype(jnp.float32)
    same = ((out_row // 2) % PLACES == in_row // NEW) & (out_row % 2 == in_row % 2)
    pieces = []
    for rr in range(RUNS):
        asked = mbuf[rr, 0] + mbuf[rr, 1] + mbuf[rr, 2] + mbuf[rr, 3]
        chosen = jnp.where(same & (asked == owner), 1.0, 0.0).astype(jnp.bfloat16)
        rows = fbuf[rr].reshape(PLACES * NEW, COLS)
        pieces.append(jnp.dot(chosen, rows, preferred_element_type=jnp.float32))
    for o in range(YS * CORES):
        rows = jnp.concatenate([piece[o * 8 : (o + 1) * 8] for piece in pieces], axis=0)
        hstage[o] = rows.astype(jnp.bfloat16)
    for step in range(1, YS * CORES):
        target = (octet + step) % (YS * CORES)
        send(
            True,
            lambda step=step, target=target: remote(
                hstage.at[target],
                hrecv.at[octet],
                h_send.at[step],
                h_recv.at[octet],
                z * (YS * CORES) + target,
            ),
        )
    hrecv[octet] = hstage[octet]
    settle()
    for step in range(1, YS * CORES):
        source = (octet + step) % (YS * CORES)
        remote(
            hstage.at[source],
            hrecv.at[source],
            h_send.at[step],
            h_recv.at[source],
            z * (YS * CORES) + source,
        ).wait_recv()
    handover_ref[...] = hrecv[...]


def local(
    new_hidden,
    new_queries,
    paged_cache,
    block_table,
    lengths,
    destination,
    train_hidden,
    train_queries,
    documents,
    project_weight,
    project_bias,
):
    vmem = pl.BlockSpec(memory_space=pltpu.VMEM)
    smem = pl.BlockSpec(memory_space=pltpu.SMEM)
    anywhere = pl.BlockSpec(memory_space=pl.ANY)
    dma = pltpu.SemaphoreType.DMA
    along = [dma((RUNS,)), dma((RUNS,)), dma((RUNS, PLACES)), dma((RUNS, PLACES))]
    decoded, attended, handed = pl.pallas_call(
        kernel,
        out_shape=(
            jax.ShapeDtypeStruct((ROWS_DEV, 2, GROUP * HEAD_DIM), jnp.bfloat16),
            jax.ShapeDtypeStruct((TRAIN_DEV, GROUP * HEAD_DIM), jnp.bfloat16),
            jax.ShapeDtypeStruct((YS * CORES, RUNS * PLACES * 2, COLS), jnp.bfloat16),
        ),
        in_specs=[smem, smem, smem, vmem, vmem, vmem, vmem] + [anywhere] * 4,
        out_specs=(vmem, vmem, vmem),
        scratch_shapes=[
            pltpu.VMEM((RUNS, PLACES, CORES, BLOCK, COLS), jnp.bfloat16),
            pltpu.VMEM((ALL_ROWS, WIDTH), jnp.bfloat16),
            pltpu.VMEM((ROWS_DEV, 2, WIDTH), jnp.bfloat16),
            pltpu.VMEM((ROWS_DEV, 2 * GROUP, HEAD_DIM), jnp.bfloat16),
            pltpu.VMEM((paged_cache.shape[0], PAGE, COLS), jnp.bfloat16),
            pltpu.VMEM((RUNS, PLACES, 1, 128), jnp.float32),
            pltpu.VMEM((RUNS, PLACES, NEW, COLS), jnp.bfloat16),
            pltpu.VMEM((RUNS, YS, ALL_ROWS, PLACES * LANES), jnp.bfloat16),
            pltpu.VMEM((YS, ALL_ROWS, COLS), jnp.float32),
            pltpu.VMEM((YS, ALL_ROWS, COLS), jnp.float32),
            pltpu.VMEM((ALL_ROWS, COLS), jnp.bfloat16),
            pltpu.VMEM((ROWS_DEV, CORES * GROUP, CONTEXT), jnp.float32),
            pltpu.VMEM((YS * CORES, RUNS * PLACES * 2, COLS), jnp.bfloat16),
            pltpu.VMEM((YS * CORES, RUNS * PLACES * 2, COLS), jnp.bfloat16),
            dma((4,)),
            *along,
            *along,
            *along,
            dma((2, RUNS + 1)),
            dma((RUNS, PLACES)),
            dma((YS, RUNS, PLACES)),
            dma((YS, RUNS, PLACES)),
            dma((2, YS)),
            dma((2, YS)),
            dma((RUNS,)),
            dma((RUNS,)),
            dma((YS * CORES,)),
            dma((YS * CORES,)),
        ],
        compiler_params=pltpu.CompilerParams(collective_id=0, has_side_effects=True),
    )(
        block_table.T,
        lengths,
        destination,
        documents,
        project_bias.reshape(1, COLS),
        new_queries,
        train_queries,
        new_hidden,
        train_hidden,
        paged_cache,
        project_weight,
    )
    handed = handed.reshape(YS * CORES, RUNS * PLACES, 2, COLS).transpose(1, 0, 2, 3)
    return decoded, attended, handed.reshape(RUNS * PLACES * YS * CORES, 2, COLS)


def solution(mesh):
    return jax.shard_map(
        local,
        mesh=mesh,
        in_specs=(
            P("fsdp", None, None),
            P("fsdp", None, "tensor"),
            P("fsdp", None, "tensor"),
            P("fsdp", None),
            P("fsdp"),
            P("fsdp"),
            P("fsdp", None),
            P("fsdp", "tensor"),
            P("fsdp", None),
            P("fsdp", "tensor"),
            P("tensor"),
        ),
        out_specs=(P("fsdp", None, "tensor"), P("fsdp", "tensor"), P("fsdp", None, "tensor")),
        check_vma=False,
    )
```

time: 101 us -> 77.2 us (0.76)
  Pallas kernels: 91.9 us -> 73 us
  local copies, waits for them, and re-layouts: 8.04 us -> 3.27 us
    pallas_call x1, Pallas kernels: 91.9 us -> 73 us  [local(): pl.pallas_call(kernel, out_shape=(jax.ShapeDtypeStruct((ROWS_DEV, 2, GROU...]
    reshape x3 -> x0, local copies, waits for them, and re-layouts: 5.07 us -> none  [the longest x1 2.03 us: local(): new_hidden.reshape(NEW, WIDTH)]
where the time goes in v2:
time: 77.2 us; the launch traced here: 77 us
  Pallas kernels  73 us (95%)
  local copies, waits for them, and re-layouts  3.27 us (4%)
    pallas_call x1, Pallas kernels, local(): pl.pallas_call(kernel, out_shape=(jax.ShapeDtypeStruct((ROWS_DEV, 2, GROU...  73 us
    unnamed x6, local copies, waits for them, and re-layouts  1.57 us

profile of v2, /device:TPU:1, one launch (start us, length us, event | category | flops | bytes accessed | tf_op | source)
XLA Modules:
  0.0 77.0 jit_solution(14972892595622000201)
XLA Ops:
  0.6 73.0 %shard_map.130 = (bf16[16,2,1024]{2,1,0:T(2,128)(2,1)}, bf16[64,1024]{1,0:T(8,128)(2,1)}, bf16[8,32,256]{2,1,0:T(8,128)(2,1)}) custom-call(s32[8,16]{1,0:T(8,128)} %bitcast.6, s32[16]{0:T(128)} %length_ref.1, s32[16]{0:T(128)} %destination_ref.1, s32[1,64]{1,0:T(1,128)} %documents_ref.1, f32[1,256]{1,0:T(1,128)} %bitcast.7, ...), custom_call_target="tpu_custom_call" | custom-call | tf_op jit(solution)/shard_map/pallas_call | solution.py:614
  73.7 1.0 %reshape.16 = bf16[8,16,2,256]{3,2,1,0:T(2,128)(2,1)S(1)} reshape(bf16[8,32,256]{2,1,0:T(8,128)(2,1)} %get-tuple-element.8) | data formatting | bytes 262144 | tf_op jit(solution)/shard_map/reshape | solution.py:667
  74.6 0.0 copy-start.1
  74.7 0.7 copy.14
  75.4 0.0 copy-start
  75.4 0.1 copy-done.1
  75.5 0.6 copy.17
  76.1 0.2 copy-done
  76.3 0.7 copy.18
Async XLA Ops:
  74.6 0.8 %copy-start.1 = (bf16[16,2,1024]{2,1,0:T(2,128)(2,1)S(1)}, bf16[16,2,1024]{2,1,0:T(2,128)(2,1)}, u32[]{:S(2)}) copy-start(bf16[16,2,1024]{2,1,0:T(2,128)(2,1)} %get-tuple-element.12) | copy-start | bytes 196612
  75.4 0.9 %copy-start = (bf16[64,1024]{1,0:T(8,128)(2,1)S(1)}, bf16[64,1024]{1,0:T(8,128)(2,1)}, u32[]{:S(2)}) copy-start(bf16[64,1024]{1,0:T(8,128)(2,1)} %get-tuple-element.13) | copy-start | bytes 393220

commit v3 on v2

--- a/solution.py
+++ b/solution.py
@@ -28,6 +28,7 @@
 NEW = ROWS_DEV * 2
 ALL_ROWS = NEW + TRAIN_DEV
 LANES = CORES * BLOCK
+NEAR = PLACES * YS * CORES
 RELAY_CHAIN = False
 RELAY_GROUP = True
 
@@ -37,6 +38,20 @@
 
 
 def kernel(
+    table_hbm,
+    length_hbm,
+    destination_hbm,
+    documents_hbm,
+    bias_hbm,
+    queries_hbm,
+    train_queries_hbm,
+    new_hidden_hbm,
+    train_hidden_hbm,
+    cache_hbm,
+    weight_hbm,
+    decoded_ref,
+    train_out_ref,
+    handover_ref,
     table_ref,
     length_ref,
     destination_ref,
@@ -44,13 +59,6 @@
     bias_ref,
     queries_ref,
     train_queries_ref,
-    new_hidden_hbm,
-    train_hidden_hbm,
-    cache_hbm,
-    weight_hbm,
-    decoded_ref,
-    train_out_ref,
-    handover_ref,
     wbuf,
     hbuf,
     raw,
@@ -72,12 +80,8 @@
     w_group_recv,
     m_chain_send,
     m_chain_recv,
-    m_group_send,
-    m_group_recv,
     f_chain_send,
     f_chain_recv,
-    f_group_send,
-    f_group_recv,
     relay_send,
     own_sem,
     y_send,
@@ -142,46 +146,53 @@
     train_copy = pltpu.make_async_copy(
         train_hidden_hbm, hbuf.at[pl.ds(NEW, TRAIN_DEV)], local_sem.at[3]
     )
+    small_copies = [
+        pltpu.make_async_copy(src, dst, local_sem.at[4 + i])
+        for i, (src, dst) in enumerate(
+            (
+                (destination_hbm, destination_ref),
+                (queries_hbm, queries_ref),
+                (table_hbm, table_ref),
+                (length_hbm, length_ref),
+                (documents_hbm, documents_ref),
+                (bias_hbm, bias_ref),
+                (train_queries_hbm, train_queries_ref),
+            )
+        )
+    ]
+    barrier = pltpu.get_barrier_semaphore()
+    here = place * (YS * CORES) + octet
+    for step in range(1, NEAR):
+        pl.semaphore_signal(
+            barrier,
+            inc=1,
+            device_id={"fsdp": run * NEAR + (here + step) % NEAR},
+            device_id_type=MESH,
+        )
+    for step in range(1, RUNS):
+        pl.semaphore_signal(
+            barrier,
+            inc=1,
+            device_id={"fsdp": ((run + step) % RUNS) * NEAR + here},
+            device_id_type=MESH,
+        )
+    expected = NEAR + RUNS - 2
     w_copy.start()
+    new_copy.start()
+    for copy in small_copies:
+        copy.start()
+    train_copy.start()
     pool_copy.start()
-    new_copy.start()
-    train_copy.start()
-
+    small_copies[0].wait()
     lane = lax.broadcasted_iota(jnp.int32, (1, 128), 1)
     wanted = jnp.zeros((1, 128), jnp.float32)
     for r in range(ROWS_DEV):
         value = (destination_ref[r] + 1).astype(jnp.float32)
-        hit = (lane // NEW == place) & ((lane % NEW) // 2 == r)
+        hit = (lane // NEW == run) & ((lane % NEW) // 2 == r)
         wanted = jnp.where(hit, value, wanted)
-    mbuf[run, place] = wanted
-
-    barrier = pltpu.get_barrier_semaphore()
-    for step in range(1, YS * CORES):
-        pl.semaphore_signal(
-            barrier,
-            inc=1,
-            device_id={"fsdp": z * (YS * CORES) + (octet + step) % (YS * CORES)},
-            device_id_type=MESH,
-        )
-    expected = jnp.int32(YS * CORES - 1)
-    near = [
-        (jnp.logical_and(run + side * far >= 0, run + side * far < RUNS), z + side * far * PLACES)
-        for far in (1, 2, 3)
-        for side in (1, -1)
-    ] + [
-        (jnp.logical_and(place + side * far >= 0, place + side * far < PLACES), z + side * far)
-        for far in (1, 2, 3)
-        for side in (1, -1)
-    ]
-    for cond, zz in near:
-
-        @pl.when(cond)
-        def _(zz=zz):
-            pl.semaphore_signal(
-                barrier, inc=1, device_id={"fsdp": device(zz, y, core)}, device_id_type=MESH
-            )
-
-        expected = expected + cond.astype(jnp.int32)
+    mbuf[run] = wanted
+
+    small_copies[1].wait()
     for r in range(ROWS_DEV):
         both_tokens = queries_ref[r]
         qbuf[r] = jnp.concatenate(
@@ -249,7 +260,7 @@
                     for side in (1, -1):
                         target = place + side * far
                         inside = both(cond, jnp.logical_and(target >= 0, target < PLACES))
-                        for block, source, _, _, gs, gr in self.parts:
+                        for block, source, _, _, gs, gr in self.parts[:1]:
                             src = source if (d == 0 and source is not None) else block(rr, place)
                             send(
                                 inside,
@@ -272,7 +283,7 @@
                         inside = both(cond, jnp.logical_and(pp >= 0, pp < PLACES))
 
                         def do(rr=rr, pp=pp):
-                            for block, _, _, _, gs, gr in self.parts:
+                            for block, _, _, _, gs, gr in self.parts[:1]:
                                 remote(
                                     block(rr, pp),
                                     block(rr, pp),
@@ -287,7 +298,7 @@
                             ahead = both(
                                 inside, jnp.logical_and(onward >= 0, onward < PLACES)
                             )
-                            for i, (block, _, _, _, _, gr) in enumerate(self.parts):
+                            for i, (block, _, _, _, _, gr) in enumerate(self.parts[:1]):
                                 send(
                                     ahead,
                                     lambda rr=rr, pp=pp, i=i, block=block, gr=gr, onward=onward: (
@@ -317,12 +328,12 @@
                 w_group_recv,
             ),
             (
-                lambda rr, pp: mbuf.at[rr, pp],
+                lambda rr, pp: mbuf.at[rr],
                 None,
                 m_chain_send,
                 m_chain_recv,
-                m_group_send,
-                m_group_recv,
+                None,
+                None,
             ),
         ],
         relay_send,
@@ -450,6 +461,8 @@
     train_copy.wait()
     hidden_out()
     pool_copy.wait()
+    for copy in small_copies[2:]:
+        copy.wait()
     old_scores(range(0, 16))
     w_copy.wait()
     chained(1)
@@ -458,26 +471,26 @@
     chained(3)
     gathered(1)
     gathered(2)
-    gathered(3)
     hidden_in()
     multiplied(0)
     multiplied(1)
+    gathered(3)
     multiplied(2)
     multiplied(3)
     shares_out(0)
     fresh = shares_in(0)
-    fbuf[run, place] = fresh
+    fbuf[run] = fresh
     kvbuf[0:NEW] = fresh
 
     rows_z = Along(
         [
             (
-                lambda rr, pp: fbuf.at[rr, pp],
+                lambda rr, pp: fbuf.at[rr],
                 None,
                 f_chain_send,
                 f_chain_recv,
-                f_group_send,
-                f_group_recv,
+                None,
+                None,
             )
         ]
     )
@@ -535,62 +548,54 @@
             train_out_ref[:, span] = result.astype(jnp.bfloat16)
 
     rows_z.start()
-    rows_z.spread(0)
     shares_out(1)
-    decode(range(0, 8))
+    decode(range(0, 16))
+    kvbuf[NEW:] = shares_in(1)
+    train(range(0, 8))
     rows_z.chain(1)
-    rows_z.spread(1)
-    decode(range(8, 14))
     rows_z.chain(2)
-    rows_z.spread(2)
-    decode(range(14, 16))
-    kvbuf[NEW:] = shares_in(1)
-    train(range(0, 4))
     rows_z.chain(3)
-    rows_z.spread(3)
-    train(range(4, 8))
-    rows_z.gather(0)
-    rows_z.gather(1)
-    rows_z.gather(2)
-    rows_z.gather(3)
-
-    out_row = lax.broadcasted_iota(jnp.int32, (64, 128), 0)
-    in_row = lax.broadcasted_iota(jnp.int32, (64, 128), 1)
-    owner = (z * (YS * CORES) + out_row // 8 + 1).astype(jnp.float32)
-    same = ((out_row // 2) % PLACES == in_row // NEW) & (out_row % 2 == in_row % 2)
-    pieces = []
-    for rr in range(RUNS):
-        asked = mbuf[rr, 0] + mbuf[rr, 1] + mbuf[rr, 2] + mbuf[rr, 3]
-        chosen = jnp.where(same & (asked == owner), 1.0, 0.0).astype(jnp.bfloat16)
-        rows = fbuf[rr].reshape(PLACES * NEW, COLS)
-        pieces.append(jnp.dot(chosen, rows, preferred_element_type=jnp.float32))
-    for o in range(YS * CORES):
-        rows = jnp.concatenate([piece[o * 8 : (o + 1) * 8] for piece in pieces], axis=0)
-        hstage[o] = rows.astype(jnp.bfloat16)
-    for step in range(1, YS * CORES):
-        target = (octet + step) % (YS * CORES)
+
+    out_row = lax.broadcasted_iota(jnp.int32, (NEAR * RUNS * 2, RUNS * NEW), 0)
+    in_row = lax.broadcasted_iota(jnp.int32, (NEAR * RUNS * 2, RUNS * NEW), 1)
+    owner = (run * NEAR + out_row // (RUNS * 2) + 1).astype(jnp.float32)
+    same = ((out_row // 2) % RUNS == in_row // NEW) & (out_row % 2 == in_row % 2)
+    asked = mbuf[0] + mbuf[1] + mbuf[2] + mbuf[3]
+    chosen = jnp.where(same & (asked == owner), 1.0, 0.0).astype(jnp.bfloat16)
+    rows = jnp.dot(
+        chosen, fbuf[...].reshape(RUNS * NEW, COLS), preferred_element_type=jnp.float32
+    )
+    hstage[...] = rows.astype(jnp.bfloat16).reshape(NEAR, RUNS, 2, COLS)
+    for step in range(NEAR - 1, 0, -1):
+        target = (here + step) % NEAR
         send(
             True,
             lambda step=step, target=target: remote(
                 hstage.at[target],
-                hrecv.at[octet],
+                hrecv.at[:, here],
                 h_send.at[step],
-                h_recv.at[octet],
-                z * (YS * CORES) + target,
+                h_recv.at[here],
+                run * NEAR + target,
             ),
         )
-    hrecv[octet] = hstage[octet]
+    hrecv[:, here] = hstage[here]
     settle()
-    for step in range(1, YS * CORES):
-        source = (octet + step) % (YS * CORES)
+    for step in range(1, NEAR):
+        source = (here + step) % NEAR
         remote(
             hstage.at[source],
-            hrecv.at[source],
+            hrecv.at[:, source],
             h_send.at[step],
             h_recv.at[source],
-            z * (YS * CORES) + source,
+            run * NEAR + source,
         ).wait_recv()
     handover_ref[...] = hrecv[...]
+
+
+def finish(decoded, attended, handed, decoded_out, attended_out, handed_out):
+    decoded_out[...] = decoded[...]
+    attended_out[...] = attended[...]
+    handed_out[...] = handed[...]
 
 
 def local(
@@ -607,7 +612,6 @@
     project_bias,
 ):
     vmem = pl.BlockSpec(memory_space=pltpu.VMEM)
-    smem = pl.BlockSpec(memory_space=pltpu.SMEM)
     anywhere = pl.BlockSpec(memory_space=pl.ANY)
     dma = pltpu.SemaphoreType.DMA
     along = [dma((RUNS,)), dma((RUNS,)), dma((RUNS, PLACES)), dma((RUNS, PLACES))]
@@ -616,29 +620,38 @@
         out_shape=(
             jax.ShapeDtypeStruct((ROWS_DEV, 2, GROUP * HEAD_DIM), jnp.bfloat16),
             jax.ShapeDtypeStruct((TRAIN_DEV, GROUP * HEAD_DIM), jnp.bfloat16),
-            jax.ShapeDtypeStruct((YS * CORES, RUNS * PLACES * 2, COLS), jnp.bfloat16),
+            jax.ShapeDtypeStruct((RUNS, NEAR, 2, COLS), jnp.bfloat16),
         ),
-        in_specs=[smem, smem, smem, vmem, vmem, vmem, vmem] + [anywhere] * 4,
+        in_specs=[anywhere] * 11,
         out_specs=(vmem, vmem, vmem),
         scratch_shapes=[
+            pltpu.SMEM((MAX_PAGES, ROWS_DEV), jnp.int32),
+            pltpu.SMEM((ROWS_DEV,), jnp.int32),
+            pltpu.SMEM((ROWS_DEV,), jnp.int32),
+            pltpu.VMEM((1, TRAIN_DEV), jnp.int32),
+            pltpu.VMEM((1, COLS), jnp.float32),
+            pltpu.VMEM((ROWS_DEV, 2, GROUP * HEAD_DIM), jnp.bfloat16),
+            pltpu.VMEM((TRAIN_DEV, GROUP * HEAD_DIM), jnp.bfloat16),
             pltpu.VMEM((RUNS, PLACES, CORES, BLOCK, COLS), jnp.bfloat16),
             pltpu.VMEM((ALL_ROWS, WIDTH), jnp.bfloat16),
             pltpu.VMEM((ROWS_DEV, 2, WIDTH), jnp.bfloat16),
             pltpu.VMEM((ROWS_DEV, 2 * GROUP, HEAD_DIM), jnp.bfloat16),
             pltpu.VMEM((paged_cache.shape[0], PAGE, COLS), jnp.bfloat16),
-            pltpu.VMEM((RUNS, PLACES, 1, 128), jnp.float32),
-            pltpu.VMEM((RUNS, PLACES, NEW, COLS), jnp.bfloat16),
+            pltpu.VMEM((RUNS, 1, 128), jnp.float32),
+            pltpu.VMEM((RUNS, NEW, COLS), jnp.bfloat16),
             pltpu.VMEM((RUNS, YS, ALL_ROWS, PLACES * LANES), jnp.bfloat16),
             pltpu.VMEM((YS, ALL_ROWS, COLS), jnp.float32),
             pltpu.VMEM((YS, ALL_ROWS, COLS), jnp.float32),
             pltpu.VMEM((ALL_ROWS, COLS), jnp.bfloat16),
             pltpu.VMEM((ROWS_DEV, CORES * GROUP, CONTEXT), jnp.float32),
-            pltpu.VMEM((YS * CORES, RUNS * PLACES * 2, COLS), jnp.bfloat16),
-            pltpu.VMEM((YS * CORES, RUNS * PLACES * 2, COLS), jnp.bfloat16),
-            dma((4,)),
+            pltpu.VMEM((NEAR, RUNS, 2, COLS), jnp.bfloat16),
+            pltpu.VMEM((RUNS, NEAR, 2, COLS), jnp.bfloat16),
+            dma((11,)),
             *along,
-            *along,
-            *along,
+            dma((RUNS,)),
+            dma((RUNS,)),
+            dma((RUNS,)),
+            dma((RUNS,)),
             dma((2, RUNS + 1)),
             dma((RUNS, PLACES)),
             dma((YS, RUNS, PLACES)),
@@ -647,8 +660,8 @@
             dma((2, YS)),
             dma((RUNS,)),
             dma((RUNS,)),
-            dma((YS * CORES,)),
-            dma((YS * CORES,)),
+            dma((NEAR,)),
+            dma((NEAR,)),
         ],
         compiler_params=pltpu.CompilerParams(collective_id=0, has_side_effects=True),
     )(
@@ -664,8 +677,15 @@
         paged_cache,
         project_weight,
     )
-    handed = handed.reshape(YS * CORES, RUNS * PLACES, 2, COLS).transpose(1, 0, 2, 3)
-    return decoded, attended, handed.reshape(RUNS * PLACES * YS * CORES, 2, COLS)
+    handed = handed.reshape(RUNS * PLACES * YS * CORES, 2, COLS)
+    return pl.pallas_call(
+        finish,
+        out_shape=tuple(
+            jax.ShapeDtypeStruct(x.shape, x.dtype) for x in (decoded, attended, handed)
+        ),
+        in_specs=[vmem] * 3,
+        out_specs=(vmem,) * 3,
+    )(decoded, attended, handed)
 
 
 def solution(mesh):

time: 77.2 us -> 73.4 us (0.951)
  local copies, waits for them, and re-layouts: 3.27 us -> 0 us
    pallas_call x1, Pallas kernels: 73 us -> 70.8 us  [local(): pl.pallas_call(kernel, out_shape=(jax.ShapeDtypeStruct((ROWS_DEV, 2, GROU...]
    pallas_call x0 -> x1, Pallas kernels: none -> 1.73 us  [local(): pl.pallas_call(finish, out_shape=tuple((jax.ShapeDtypeStruct(x.shape, x.d...]
    unnamed x6 -> x0, local copies, waits for them, and re-layouts: 1.57 us -> none
    reshape x1 -> x0, local copies, waits for them, and re-layouts: 0.96 us -> none  [local(): handed.reshape(YS * CORES, RUNS * PLACES, 2, COLS).transpose(1, 0, 2, 3)]
where the time goes in v3:
time: 73.4 us; the launch traced here: 73.2 us
  Pallas kernels  72.5 us (99%)
    pallas_call x1, Pallas kernels, local(): pl.pallas_call(kernel, out_shape=(jax.ShapeDtypeStruct((ROWS_DEV, 2, GROU...  70.8 us
    pallas_call x1, Pallas kernels, local(): pl.pallas_call(finish, out_shape=tuple((jax.ShapeDtypeStruct(x.shape, x.d...  1.73 us

profile of v3, /device:TPU:1, one launch (start us, length us, event | category | flops | bytes accessed | tf_op | source)
XLA Modules:
  0.0 73.2 jit_solution(15352923511736742804)
XLA Ops:
  0.6 70.8 %shard_map.130 = (bf16[16,2,1024]{2,1,0:T(2,128)(2,1)}, bf16[64,1024]{1,0:T(8,128)(2,1)}, bf16[4,32,2,256]{3,2,1,0:T(2,128)(2,1)}) custom-call(s32[8,16]{1,0:T(8,128)} %bitcast.4, s32[16]{0:T(128)} %length_hbm.1, s32[16]{0:T(128)} %destination_hbm.1, s32[1,64]{1,0:T(1,128)} %documents_hbm.1, f32[1,256]{1,0:T(1,128)} %bitcast.5, ...), custom_call_target="tpu_custom_call" | custom-call | tf_op jit(solution)/shard_map/pallas_call | solution.py:618
  71.4 1.7 %shard_map.131 = (bf16[16,2,1024]{2,1,0:T(2,128)(2,1)}, bf16[64,1024]{1,0:T(8,128)(2,1)}, bf16[128,2,256]{2,1,0:T(2,128)(2,1)}) custom-call(bf16[16,2,1024]{2,1,0:T(2,128)(2,1)} %get-tuple-element.6.decoded, bf16[64,1024]{1,0:T(8,128)(2,1)} %get-tuple-element.7.attended, bf16[128,2,256]{2,1,0:T(2,128)(2,1)} %bitcast.3), custom_call_target="tpu_custom_call" | custom-call | tf_op jit(solution)/shard_map/pallas_call | solution.py:681

commit v4 on v3

--- a/solution.py
+++ b/solution.py
@@ -134,10 +134,9 @@
         when(cond, lambda: make().start())
         pending.append((cond, make))
 
-    def settle():
-        for cond, make in pending:
+    def settle(batch):
+        for cond, make in batch:
             when(cond, lambda make=make: make().wait_send())
-        pending.clear()
 
     own_w = wbuf.at[run, place, core]
     w_copy = pltpu.make_async_copy(weight_hbm, own_w, local_sem.at[0])
@@ -208,7 +207,7 @@
             self.relay = relay
 
         def start(self):
-            for far in (2, 1) if self.relay is not None and RELAY_CHAIN else (3, 2, 1):
+            for far in (1, 2, 3) if self.relay is not None else (3, 2, 1):
                 for side in (1, -1):
                     target = run + side * far
                     cond = jnp.logical_and(target >= 0, target < RUNS)
@@ -547,11 +546,14 @@
             )
             train_out_ref[:, span] = result.astype(jnp.bfloat16)
 
+    weight_sends = list(pending)
+    pending.clear()
     rows_z.start()
     shares_out(1)
     decode(range(0, 16))
     kvbuf[NEW:] = shares_in(1)
     train(range(0, 8))
+    settle(weight_sends)
     rows_z.chain(1)
     rows_z.chain(2)
     rows_z.chain(3)
@@ -579,7 +581,6 @@
             ),
         )
     hrecv[:, here] = hstage[here]
-    settle()
     for step in range(1, NEAR):
         source = (here + step) % NEAR
         remote(
@@ -590,6 +591,7 @@
             run * NEAR + source,
         ).wait_recv()
     handover_ref[...] = hrecv[...]
+    settle(pending)
 
 
 def finish(decoded, attended, handed, decoded_out, attended_out, handed_out):
@@ -612,7 +614,7 @@
     project_bias,
 ):
     vmem = pl.BlockSpec(memory_space=pltpu.VMEM)
-    anywhere = pl.BlockSpec(memory_space=pl.ANY)
+    hbm = pl.BlockSpec(memory_space=pltpu.HBM)
     dma = pltpu.SemaphoreType.DMA
     along = [dma((RUNS,)), dma((RUNS,)), dma((RUNS, PLACES)), dma((RUNS, PLACES))]
     decoded, attended, handed = pl.pallas_call(
@@ -622,7 +624,7 @@
             jax.ShapeDtypeStruct((TRAIN_DEV, GROUP * HEAD_DIM), jnp.bfloat16),
             jax.ShapeDtypeStruct((RUNS, NEAR, 2, COLS), jnp.bfloat16),
         ),
-        in_specs=[anywhere] * 11,
+        in_specs=[hbm] * 11,
         out_specs=(vmem, vmem, vmem),
         scratch_shapes=[
             pltpu.SMEM((MAX_PAGES, ROWS_DEV), jnp.int32),
@@ -663,19 +665,26 @@
             dma((NEAR,)),
             dma((NEAR,)),
         ],
-        compiler_params=pltpu.CompilerParams(collective_id=0, has_side_effects=True),
+        compiler_params=pltpu.CompilerParams(
+            collective_id=0, has_side_effects=True, vmem_limit_bytes=24 * 1024 * 1024
+        ),
     )(
-        block_table.T,
-        lengths,
-        destination,
-        documents,
-        project_bias.reshape(1, COLS),
-        new_queries,
-        train_queries,
-        new_hidden,
-        train_hidden,
-        paged_cache,
-        project_weight,
+        *(
+            pltpu.with_memory_space_constraint(x, pltpu.HBM)
+            for x in (
+                block_table.T,
+                lengths,
+                destination,
+                documents,
+                project_bias.reshape(1, COLS),
+                new_queries,
+                train_queries,
+                new_hidden,
+                train_hidden,
+                paged_cache,
+                project_weight,
+            )
+        )
     )
     handed = handed.reshape(RUNS * PLACES * YS * CORES, 2, COLS)
     return pl.pallas_call(
@@ -685,6 +694,7 @@
         ),
         in_specs=[vmem] * 3,
         out_specs=(vmem,) * 3,
+        compiler_params=pltpu.CompilerParams(vmem_limit_bytes=4 * 1024 * 1024),
     )(decoded, attended, handed)
 
 

time: 73.4 us -> 71.8 us (0.978)
  Pallas kernels: 72.5 us -> 71 us
    pallas_call x1, Pallas kernels: 1.73 us -> 0.74 us  [local(): pl.pallas_call(finish, out_shape=tuple((jax.ShapeDtypeStruct(x.shape, x.d...]
where the time goes in v4:
time: 71.8 us; the launch traced here: 71.6 us
  Pallas kernels  71 us (99%)
    pallas_call x1, Pallas kernels, local(): pl.pallas_call(kernel, out_shape=(jax.ShapeDtypeStruct((ROWS_DEV, 2, GROU...  70.2 us

profile of v4, /device:TPU:1, one launch (start us, length us, event | category | flops | bytes accessed | tf_op | source)
XLA Modules:
  0.0 71.6 jit_solution(5750054798292911672)
XLA Ops:
  0.6 70.2 %shard_map.130 = (bf16[16,2,1024]{2,1,0:T(2,128)(2,1)S(1)}, bf16[64,1024]{1,0:T(8,128)(2,1)S(1)}, bf16[4,32,2,256]{3,2,1,0:T(2,128)(2,1)S(1)}) custom-call(s32[8,16]{1,0:T(8,128)} %bitcast.4, s32[16]{0:T(128)} %length_hbm.1, s32[16]{0:T(128)} %destination_hbm.1, s32[1,64]{1,0:T(1,128)} %documents_hbm.1, f32[1,256]{1,0:T(1,128)} %bitcast.5, ...), custom_call_target="tpu_custom_call" | custom-call | tf_op jit(solution)/shard_map/pallas_call | solution.py:620
  70.9 0.7 %shard_map.131 = (bf16[16,2,1024]{2,1,0:T(2,128)(2,1)}, bf16[64,1024]{1,0:T(8,128)(2,1)}, bf16[128,2,256]{2,1,0:T(2,128)(2,1)}) custom-call(bf16[16,2,1024]{2,1,0:T(2,128)(2,1)S(1)} %get-tuple-element.6.decoded, bf16[64,1024]{1,0:T(8,128)(2,1)S(1)} %get-tuple-element.7.attended, bf16[128,2,256]{2,1,0:T(2,128)(2,1)S(1)} %bitcast.3), custom_call_target="tpu_custom_call" | custom-call | tf_op jit(solution)/shard_map/pallas_call | solution.py:690

commit v5 on v4

--- a/solution.py
+++ b/solution.py
@@ -473,8 +473,8 @@
     hidden_in()
     multiplied(0)
     multiplied(1)
+    multiplied(2)
     gathered(3)
-    multiplied(2)
     multiplied(3)
     shares_out(0)
     fresh = shares_in(0)
@@ -554,16 +554,15 @@
     kvbuf[NEW:] = shares_in(1)
     train(range(0, 8))
     settle(weight_sends)
-    rows_z.chain(1)
-    rows_z.chain(2)
-    rows_z.chain(3)
-
     out_row = lax.broadcasted_iota(jnp.int32, (NEAR * RUNS * 2, RUNS * NEW), 0)
     in_row = lax.broadcasted_iota(jnp.int32, (NEAR * RUNS * 2, RUNS * NEW), 1)
     owner = (run * NEAR + out_row // (RUNS * 2) + 1).astype(jnp.float32)
     same = ((out_row // 2) % RUNS == in_row // NEW) & (out_row % 2 == in_row % 2)
     asked = mbuf[0] + mbuf[1] + mbuf[2] + mbuf[3]
     chosen = jnp.where(same & (asked == owner), 1.0, 0.0).astype(jnp.bfloat16)
+    rows_z.chain(1)
+    rows_z.chain(2)
+    rows_z.chain(3)
     rows = jnp.dot(
         chosen, fbuf[...].reshape(RUNS * NEW, COLS), preferred_element_type=jnp.float32
     )

time: 71.8 us -> 71.7 us (level)
  no operation moved by 1% of the time
where the time goes in v5:
time: 71.7 us; the launch traced here: 71.6 us
  Pallas kernels  70.9 us (99%)
    pallas_call x1, Pallas kernels, local(): pl.pallas_call(kernel, out_shape=(jax.ShapeDtypeStruct((ROWS_DEV, 2, GROU...  70.2 us

profile of v5, /device:TPU:1, one launch (start us, length us, event | category | flops | bytes accessed | tf_op | source)
XLA Modules:
  0.0 71.6 jit_solution(636456662299430798)
XLA Ops:
  0.6 70.2 %shard_map.130 = (bf16[16,2,1024]{2,1,0:T(2,128)(2,1)S(1)}, bf16[64,1024]{1,0:T(8,128)(2,1)S(1)}, bf16[4,32,2,256]{3,2,1,0:T(2,128)(2,1)S(1)}) custom-call(s32[8,16]{1,0:T(8,128)} %bitcast.4, s32[16]{0:T(128)} %length_hbm.1, s32[16]{0:T(128)} %destination_hbm.1, s32[1,64]{1,0:T(1,128)} %documents_hbm.1, f32[1,256]{1,0:T(1,128)} %bitcast.5, ...), custom_call_target="tpu_custom_call" | custom-call | tf_op jit(solution)/shard_map/pallas_call | solution.py:619
  70.8 0.7 %shard_map.131 = (bf16[16,2,1024]{2,1,0:T(2,128)(2,1)}, bf16[64,1024]{1,0:T(8,128)(2,1)}, bf16[128,2,256]{2,1,0:T(2,128)(2,1)}) custom-call(bf16[16,2,1024]{2,1,0:T(2,128)(2,1)S(1)} %get-tuple-element.6.decoded, bf16[64,1024]{1,0:T(8,128)(2,1)S(1)} %get-tuple-element.7.attended, bf16[128,2,256]{2,1,0:T(2,128)(2,1)S(1)} %bitcast.3), custom_call_target="tpu_custom_call" | custom-call | tf_op jit(solution)/shard_map/pallas_call | solution.py:689
